TPU v7x, 512 devices: a whole 4x8x8 slice. The times are simulated.
512 devices in a mesh: ao: 32 (over x, z), ri: 16 (over y, core).
Axes of the slice: x: 4, y: 8, z: 8, core: 2. Of those that a mesh axis runs over, the one named last changes fastest.
Arguments:
- three_center: bfloat16 [256, 12288, 128], P('ri', 'ao'), may hold values from -0.19921875 to 0.19921875
- occ_band: bfloat16 [4096, 640], P('ao'), may hold values from -0.3125 to 0.3125
- virt_band: bfloat16 [4096, 384], P('ao'), may hold values from -0.3125 to 0.3125
- three_mask: int32 [32, 3], P('ao'), may hold values 0 or 1
- occ_mask: int32 [32, 5], P('ao'), may hold values 0 or 1
- virt_mask: int32 [32, 3], P('ao'), may hold values 0 or 1
Outputs:
- chi: float32 [256, 256], P('ri')
All inputs are finite; a program needn't handle non-finite values. No bound on the sum of `three_mask` or of `occ_mask` or of `virt_mask` on one device may be relied on, other than what follows from the above.
Results may differ from a plain program's by a relative error of at most 0.004.
Values may be sent and summed in bfloat16 or wider, within the bound.
A program may use at most 64 MiB of HBM per device.

v0:
```python
import jax
import jax.numpy as jnp
from jax import lax
from jax.sharding import PartitionSpec as P


def padded_2(value, sides, width):
    for axis, dim in sides:
        peers, length = (lax.axis_size(axis), value.shape[dim])
        up = [(i, (i + 1) % peers) for i in range(peers)]
        down = [(j, i) for i, j in up]
        last = lax.slice_in_dim(value, length - width, length, axis=dim)
        initial = lax.slice_in_dim(value, 0, width, axis=dim)
        before = lax.ppermute(last, axis, up)
        after = lax.ppermute(initial, axis, down)
        value = jnp.concatenate([before, value, after], axis=dim)
    return value


def per_device(three_center, occ_band, virt_band, three_mask, occ_mask, virt_mask):
    tile_size = occ_band.shape[0]
    local_rows = three_center.shape[0]
    live_b = (
        three_center.reshape(local_rows, 3, tile_size, tile_size)
        * three_mask[0].astype(three_center.dtype)[None, :, None, None]
    )
    live_b = live_b.reshape(local_rows, 3 * tile_size, tile_size)
    live_occ = occ_band * jnp.repeat(occ_mask[0].astype(occ_band.dtype), tile_size)[None, :]
    live_virt = virt_band * jnp.repeat(virt_mask[0].astype(virt_band.dtype), tile_size)[None, :]
    occ_rows = padded_2(live_occ, (("ao", 0),), tile_size)
    blank = jnp.zeros((tile_size, tile_size), occ_band.dtype)
    green_block = jnp.concatenate(
        [
            jnp.concatenate([occ_rows[0:tile_size, tile_size:], blank], 1),
            occ_rows[tile_size : 2 * tile_size],
            jnp.concatenate([blank, occ_rows[2 * tile_size :, : 4 * tile_size]], 1),
        ],
        0,
    )
    m_local = jnp.einsum(
        "ml,pmn->pln", green_block, live_b, preferred_element_type=jnp.float32
    ).astype(jnp.bfloat16)
    padded = padded_2(m_local, (("ao", 2),), tile_size)
    needed = jnp.concatenate(
        [
            padded[:, 2 * tile_size : 5 * tile_size, 0:tile_size],
            padded[:, tile_size : 4 * tile_size, tile_size : 2 * tile_size],
            padded[:, 0 : 3 * tile_size, 2 * tile_size : 3 * tile_size],
        ],
        2,
    )
    product = jnp.einsum(
        "plv,sv->pls", needed, live_virt, preferred_element_type=jnp.float32
    ).astype(jnp.bfloat16)
    product_flat = product.reshape(local_rows, 3 * tile_size * tile_size)
    b_flat = live_b.reshape(local_rows, 3 * tile_size * tile_size)
    product_all, b_all = (
        lax.all_to_all(product_flat, "ri", split_axis=1, concat_axis=0, tiled=True),
        lax.all_to_all(b_flat, "ri", split_axis=1, concat_axis=0, tiled=True),
    )
    partial_chi = lax.dot_general(
        product_all, b_all, (((1,), (1,)), ((), ())), preferred_element_type=jnp.float32
    )
    row_panel = lax.psum_scatter(partial_chi, "ri", scatter_dimension=0, tiled=True)
    summed = lax.psum(row_panel, "ao")
    return -summed


def solution(mesh):
    placed = (
        P("ri", "ao", None),
        P("ao", None),
        P("ao", None),
        P("ao", None),
        P("ao", None),
        P("ao", None),
    )
    return jax.shard_map(
        per_device, mesh=mesh, in_specs=placed, out_specs=P("ri", None), check_vma=False
    )
```

profile of v0, /device:TPU:32, one launch (start us, length us, event | category | flops | bytes accessed | tf_op | source)
XLA Modules:
  0.0 353.9 jit_solution(3540133267525671056)
XLA Ops:
  6.5 0.7 convert_bitcast_fusion.2
  7.2 0.1 broadcast_bitcast_fusion
  7.3 0.9 broadcast_multiply_fusion.1
  8.2 4.3 %collective-permute-start = (bf16[128,640]{1,0:T(8,128)(2,1)S(1)}, bf16[128,640]{1,0:T(8,128)(2,1)}, u32[]{:S(2)}, u32[]{:S(2)}) collective-permute-start(bf16[128,640]{1,0:T(8,128)(2,1)S(1)} %broadcast_multiply_fusion.1), channel_id=1, source_target_pairs={{0,16},{16,32},{32,48},{48,64},{64,80},{80,96},{96,112},{112,128},... | collective-permute-start | bytes 491528 | tf_op jit(solution)/shard_map/ppermute | solution.py:14
  12.5 10.8 %collective-permute-start.1 = (bf16[128,640]{1,0:T(8,128)(2,1)S(1)}, bf16[128,640]{1,0:T(8,128)(2,1)}, u32[]{:S(2)}, u32[]{:S(2)}) collective-permute-start(bf16[128,640]{1,0:T(8,128)(2,1)S(1)} %broadcast_multiply_fusion.1), channel_id=1, source_target_pairs={{16,0},{32,16},{48,32},{64,48},{80,64},{96,80},{112,96},{128,112},... | collective-permute-start | bytes 491528 | tf_op jit(solution)/shard_map/ppermute | solution.py:15
  23.3 0.7 convert_bitcast_fusion.3
  23.9 0.1 mul.53
  24.1 0.0 copy-start
  24.1 2.7 reshape.31
  26.8 0.1 broadcast_bitcast_fusion.2
  26.9 0.0 collective-permute-done
  26.9 0.9 slice.20
  27.8 0.0 collective-permute-done.1
  27.8 0.9 slice.21
  28.7 0.0 copy-done
  28.7 3.3 convert_bitcast_fusion
  32.0 1.9 collective-permute-start.2
  34.0 7.2 %collective-permute-start.3 = (bf16[16,640,128]{1,2,0:T(8,128)(2,1)}, bf16[16,640,128]{1,2,0:T(8,128)(2,1)}, u32[]{:S(2)}, u32[]{:S(2)}) collective-permute-start(bf16[16,640,128]{1,2,0:T(8,128)(2,1)} %convert_bitcast_fusion), channel_id=1, source_target_pairs={{16,0},{32,16},{48,32},{64,48},{80,64},{96,80},{112,96},{128,112},... | collective-permute-start | bytes 7864328 | tf_op jit(solution)/shard_map/ppermute | solution.py:15
  41.2 0.1 broadcast_multiply_fusion
  41.3 2.0 copy.19
  43.4 0.0 copy-start.2
  43.4 7.4 %all-to-all-start.1 = ((bf16[16,16,3072]{2,0,1:T(8,128)(2,1)}), bf16[16,16,3072]{2,0,1:T(8,128)(2,1)}, u32[]{:S(2)}, u32[]{:S(2)}) async-start(bf16[16,16,3072]{2,0,1:T(8,128)(2,1)} %copy.19), calls=%async_computation.1 | async-start | bytes 3145728 | tf_op jit(solution)/shard_map/all_to_all | solution.py:59
  50.7 0.0 reduce-scatter.2.cloned.1.call-start
  50.8 0.0 copy-done.2
  50.8 0.1 broadcast_bitcast_fusion.1
  50.9 1.6 slice.23
  52.5 43.4 %collective-permute-done.2 = bf16[16,640,128]{1,2,0:T(8,128)(2,1)} collective-permute-done((bf16[16,640,128]{1,2,0:T(8,128)(2,1)}, bf16[16,640,128]{1,2,0:T(8,128)(2,1)}, u32[]{:S(2)}, u32[]{:S(2)}) %collective-permute-start.2) | collective-permute-done | bytes 2621472 | tf_op jit(solution)/shard_map/ppermute | solution.py:14
  95.9 1.6 slice.22
  97.5 0.0 copy-start.1
  97.5 0.0 collective-permute-done.3
  97.5 1.6 slice.24
  99.1 0.0 copy-done.1
  99.2 1.7 fusion.6
  100.8 0.7 all_to_all.26
  101.5 0.9 copy.18
  102.4 0.0 all-to-all-done.1
  102.4 42.5 %all_to_all.35 = bf16[16,16,3072]{2,0,1:T(8,128)(2,1)S(1)} all-to-all(bf16[16,16,3072]{2,0,1:T(8,128)(2,1)S(1)} %copy.18), channel_id=1, replica_groups=mesh['ao'=32,'ri'=16] {'ri'}, dimensions={1} | all-to-all | bytes 3145728 | tf_op jit(solution)/shard_map/all_to_all | solution.py:58
  144.9 2.7 fusion.32
  147.6 0.0 reduce-scatter.2.cloned.1.call-update
  147.6 55.1 %reduce-scatter.2.cloned.1.call-done = f32[16,256]{1,0:T(8,128)} async-done(((f32[256,256]{1,0:T(8,128)}), f32[16,256]{1,0:T(8,128)}) %reduce-scatter.2.cloned.1.call-update) | async-done | bytes 16400 | tf_op jit(solution)/shard_map/reduce_scatter | solution.py:64
  202.8 143.7 %psum.7 = f32[16,256]{1,0:T(8,128)S(1)} all-reduce(f32[16,256]{1,0:T(8,128)} %reduce-scatter.2.cloned.1.call-done), channel_id=1, replica_groups=mesh['ao'=32,'ri'=16] {'ao'}, use_global_device_ids=true, to_apply=%region_1.0 | all-reduce | flops 4096 | bytes 32768 | tf_op jit(solution)/shard_map/psum | solution.py:65
  346.5 0.6 neg.3
  (2 shorter events, 0.1 us)
Async XLA Ops:
  8.2 18.7 %collective-permute-start = (bf16[128,640]{1,0:T(8,128)(2,1)S(1)}, bf16[128,640]{1,0:T(8,128)(2,1)}, u32[]{:S(2)}, u32[]{:S(2)}) collective-permute-start(bf16[128,640]{1,0:T(8,128)(2,1)S(1)} %broadcast_multiply_fusion.1), channel_id=1, source_target_pairs={{0,16},{16,32},{32,48},{48,64},{64,80},{80,96},{96,112},{112,128},... | collective-permute-start | bytes 491528 | tf_op jit(solution)/shard_map/ppermute | solution.py:14
  12.5 15.3 %collective-permute-start.1 = (bf16[128,640]{1,0:T(8,128)(2,1)S(1)}, bf16[128,640]{1,0:T(8,128)(2,1)}, u32[]{:S(2)}, u32[]{:S(2)}) collective-permute-start(bf16[128,640]{1,0:T(8,128)(2,1)S(1)} %broadcast_multiply_fusion.1), channel_id=1, source_target_pairs={{16,0},{32,16},{48,32},{64,48},{80,64},{96,80},{112,96},{128,112},... | collective-permute-start | bytes 491528 | tf_op jit(solution)/shard_map/ppermute | solution.py:15
  24.1 4.6 %copy-start = (bf16[16,384,128]{2,1,0:T(8,128)(2,1)S(1)}, bf16[16,384,128]{2,1,0:T(8,128)(2,1)}, u32[]{:S(2)}) copy-start(bf16[16,384,128]{2,1,0:T(8,128)(2,1)} %param.6) | copy-start | bytes 4718596
  32.0 63.8 %collective-permute-start.2 = (bf16[16,640,128]{1,2,0:T(8,128)(2,1)}, bf16[16,640,128]{1,2,0:T(8,128)(2,1)}, u32[]{:S(2)}, u32[]{:S(2)}) collective-permute-start(bf16[16,640,128]{1,2,0:T(8,128)(2,1)} %convert_bitcast_fusion), channel_id=1, source_target_pairs={{0,16},{16,32},{32,48},{48,64},{64,80},{80,96},{96,112},{112,128},... | collective-permute-start | bytes 7864328 | tf_op jit(solution)/shard_map/ppermute | solution.py:14
  34.0 63.5 %collective-permute-start.3 = (bf16[16,640,128]{1,2,0:T(8,128)(2,1)}, bf16[16,640,128]{1,2,0:T(8,128)(2,1)}, u32[]{:S(2)}, u32[]{:S(2)}) collective-permute-start(bf16[16,640,128]{1,2,0:T(8,128)(2,1)} %convert_bitcast_fusion), channel_id=1, source_target_pairs={{16,0},{32,16},{48,32},{64,48},{80,64},{96,80},{112,96},{128,112},... | collective-permute-start | bytes 7864328 | tf_op jit(solution)/shard_map/ppermute | solution.py:15
  43.4 7.4 %copy-start.2 = (s32[1,3]{1,0:T(1,128)S(1)}, s32[1,3]{1,0:T(1,128)}, u32[]{:S(2)}) copy-start(s32[1,3]{1,0:T(1,128)} %param.11) | copy-start | bytes 40
  43.4 59.0 %all-to-all-start.1 = ((bf16[16,16,3072]{2,0,1:T(8,128)(2,1)}), bf16[16,16,3072]{2,0,1:T(8,128)(2,1)}, u32[]{:S(2)}, u32[]{:S(2)}) async-start(bf16[16,16,3072]{2,0,1:T(8,128)(2,1)} %copy.19), calls=%async_computation.1 | async-start | bytes 3145728 | tf_op jit(solution)/shard_map/all_to_all | solution.py:59
  50.7 152.0 %reduce-scatter.2.cloned.1.call-start = ((), (), s32[]{:S(2)}) async-start(), calls=%async_computation.3 | async-start | bytes 278528 | tf_op jit(solution)/shard_map/reduce_scatter | solution.py:64
  97.5 1.7 copy-start.1
Sparse Core Ops, SparseCore 0:
  147.8 54.9 reduce-scatter.1
where the time goes:
time: 354 us
  blocking collectives  186 us (53%)
  waiting for transfers between devices  98.6 us (28%)
  starting transfers between devices  31.6 us (9%)
  between operations  13.6 us (4%)
  local copies, waits for them, and re-layouts  13.3 us (4%)
  matrix products  7.72 us (2%)
    psum x1, blocking collectives, per_device(): summed = lax.psum(row_panel, 'ao')  144 us
    reduce_scatter x1, waiting for transfers between devices, per_device(): lax.psum_scatter(partial_chi, 'ri', scatter_dimension=0, tiled=True)  55.1 us
    ppermute x2, waiting for transfers between devices, padded_2(): before = lax.ppermute(last, axis, up)  43.4 us
    all_to_all x1, blocking collectives, per_device(): lax.all_to_all(product_flat, 'ri', split_axis=1, concat_axis=0, tiled=True)  42.5 us
    ppermute x2, starting transfers between devices, padded_2(): after = lax.ppermute(initial, axis, down)  18 us
    all_to_all x1, starting transfers between devices, per_device(): lax.all_to_all(b_flat, 'ri', split_axis=1, concat_axis=0, tiled=True)  7.36 us
  transfers between devices with their start and end apart: 6, of which 2 were waited for; matrix products, arithmetic and copies ran while one was open for 4% of the time, Pallas kernels for 0%

commit v1 on v0

v1 whole, which is shorter than its diff:
```python
import functools

import jax
import jax.numpy as jnp
from jax import lax
from jax.experimental import pallas as pl
from jax.experimental.pallas import tpu as pltpu
from jax.sharding import PartitionSpec as P

MESH = pl.DeviceIdType.MESH
F32 = jnp.float32
BF16 = jnp.bfloat16


def kernel(
    n_ao, n_ri, n_x, n_z, tile, rows,
    b_ref, occ_ref, virt_ref, tm_ref, om_ref, vm_ref, o_ref,
    wide, bt, occ_own, occ_left, occ_right, green, virt, m_buf, m_left, m_right,
    nt, b_all, n_all, acc, panels, own_x, own_z,
    occ_ss, occ_rs, m_ss, m_rs, b_ss, b_rs, n_ss, n_rs, p_ss, p_rs, x_ss, x_rs, z_ss, z_rs,
):
    ao = lax.axis_index("ao")
    ri = lax.axis_index("ri")
    x, z = ao // n_z, lax.rem(ao, n_z)
    right, left = lax.rem(ao + 1, n_ao), lax.rem(ao + n_ao - 1, n_ao)
    share = tile // n_ri

    def remote(src, dst, ss, rs, where):
        return pltpu.make_async_remote_copy(
            src_ref=src, dst_ref=dst, send_sem=ss, recv_sem=rs, device_id=where, device_id_type=MESH
        )

    def ri_peer(d):
        return lax.rem(ri + d, n_ri)

    def x_peer(d):
        return lax.rem(x + d, n_x) * n_z + z

    def z_peer(d):
        return x * n_z + lax.rem(z + d, n_z)

    barrier = pltpu.get_barrier_semaphore()

    def greet(where):
        pl.semaphore_signal(barrier, inc=1, device_id=where, device_id_type=MESH)

    greet({"ao": right})
    greet({"ao": left})

    def greet_ri(d, carry):
        greet({"ri": ri_peer(d)})
        return carry

    lax.fori_loop(1, n_ri, greet_ri, 0)
    for d in range(1, n_z):
        greet({"ao": z_peer(d)})
    for d in range(1, n_x):
        greet({"ao": x_peer(d)})

    for j in range(5):
        cols = pl.ds(j * tile, tile)
        occ_own[:, cols] = (occ_ref[:, cols].astype(F32) * om_ref[0, j].astype(F32)).astype(BF16)
    for j in range(3):
        cols = pl.ds(j * tile, tile)
        virt[:, cols] = (virt_ref[:, cols].astype(F32) * vm_ref[0, j].astype(F32)).astype(BF16)

    def regroup(source_rows, stride, target, lam0):
        def body(l, carry):
            target[lam0 + l] = source_rows[pl.ds(l, rows, stride=stride), :].astype(BF16)
            return carry

        lax.fori_loop(0, tile, body, 0, unroll=8)

    def widen_b(j):
        flag = tm_ref[0, j].astype(F32)

        def body(p, carry):
            wide[pl.ds(pl.multiple_of(p * tile, tile), tile), :] = (
                b_ref[p, pl.ds(j * tile, tile), :].astype(F32) * flag
            )
            return carry

        lax.fori_loop(0, rows, body, 0)

    widen_b(0)
    regroup(wide, tile, bt, 0)

    pl.semaphore_wait(barrier, 2 + n_ri - 1 + n_z - 1 + n_x - 1)

    to_right = remote(occ_own.at[:, pl.ds(tile, 4 * tile)], occ_left, occ_ss.at[0], occ_rs.at[0], {"ao": right})
    to_left = remote(occ_own.at[:, pl.ds(0, 4 * tile)], occ_right, occ_ss.at[1], occ_rs.at[1], {"ao": left})
    to_right.start()
    to_left.start()

    def share_copy(source, target, ss, rs, j, d):
        peer = ri_peer(d)
        return remote(
            source.at[pl.ds(pl.multiple_of(j * tile + peer * share, share), share)],
            target.at[j, ri],
            ss.at[j, d],
            rs.at[j, d],
            {"ri": peer},
        )

    def spread(source, target, ss, rs, j):
        def body(d, carry):
            share_copy(source, target, ss, rs, j, d).start()
            return carry

        lax.fori_loop(1, n_ri, body, 0)
        target[j, ri] = source[pl.ds(pl.multiple_of(j * tile + ri * share, share), share)]

    def arrive(source, target, ss, rs, j):
        def body(d, carry):
            share_copy(source, target, ss, rs, j, d).wait_recv()
            return carry

        lax.fori_loop(1, n_ri, body, 0)

    def drain(source, target, ss, rs, j):
        def body(d, carry):
            share_copy(source, target, ss, rs, j, d).wait_send()
            return carry

        lax.fori_loop(1, n_ri, body, 0)

    spread(bt, b_all, b_ss, b_rs, 0)

    to_right.wait_recv()
    to_left.wait_recv()
    for i, (band, shift) in enumerate(((occ_left, 0), (occ_own, 0), (occ_right, -1))):
        flag = tm_ref[0, i].astype(F32)
        for j in range(5):
            k = j + shift
            if 0 <= k < band.shape[1] // tile:
                block = band[:, pl.ds(k * tile, tile)].astype(F32) * flag
                green[pl.ds(j * tile, tile), pl.ds(i * tile, tile)] = block.T.astype(BF16)
            else:
                green[pl.ds(j * tile, tile), pl.ds(i * tile, tile)] = jnp.zeros((tile, tile), BF16)

    def make_m(first, count):
        lhs_rows = pl.ds(first * tile, count * tile)

        def body(q, carry):
            pair = jnp.concatenate([b_ref[2 * q], b_ref[2 * q + 1]], axis=1)
            got = jnp.dot(green[lhs_rows, :], pair, preferred_element_type=F32).astype(BF16)
            m_buf[2 * q, lhs_rows, :] = got[:, :tile]
            m_buf[2 * q + 1, lhs_rows, :] = got[:, tile:]
            return carry

        lax.fori_loop(0, rows // 2, body, 0)

    def m_copies(j):
        cols = pl.ds(j * tile, tile)
        return (
            remote(m_buf.at[:, pl.ds((j + 2) * tile, tile), :], m_left.at[:, cols, :], m_ss.at[0, j], m_rs.at[0, j], {"ao": right}),
            remote(m_buf.at[:, cols, :], m_right.at[:, cols, :], m_ss.at[1, j], m_rs.at[1, j], {"ao": left}),
        )

    make_m(0, 3)
    for copy in m_copies(0):
        copy.start()
    make_m(3, 1)
    for copy in m_copies(1):
        copy.start()
    make_m(4, 1)
    for copy in m_copies(2):
        copy.start()

    for j in (1, 2):
        widen_b(j)
        regroup(wide, tile, bt, j * tile)
        spread(bt, b_all, b_ss, b_rs, j)

    for j in range(3):
        for copy in m_copies(j):
            copy.wait_recv()

        def n_body(p, carry, j=j):
            needed = jnp.concatenate(
                [
                    m_left[p, pl.ds(j * tile, tile), :],
                    m_buf[p, pl.ds((j + 1) * tile, tile), :],
                    m_right[p, pl.ds(j * tile, tile), :],
                ],
                axis=1,
            )
            wide[pl.ds(pl.multiple_of(p * tile, tile), tile), :] = lax.dot_general(
                needed, virt[...], (((1,), (1,)), ((), ())), preferred_element_type=F32
            )
            return carry

        lax.fori_loop(0, rows, n_body, 0)
        regroup(wide, tile, nt, j * tile)
        spread(nt, n_all, n_ss, n_rs, j)

    acc[...] = jnp.zeros_like(acc)
    for j in range(3):
        arrive(bt, b_all, b_ss, b_rs, j)
        arrive(nt, n_all, n_ss, n_rs, j)
        total = acc[...]
        for l in range(0, share, 2):
            size = n_ri * rows

            def pair_of(ref):
                return jnp.concatenate(
                    [ref[j, :, l].reshape(size, tile), ref[j, :, l + 1].reshape(size, tile)], axis=1
                )

            total = total + lax.dot_general(
                pair_of(n_all), pair_of(b_all), (((1,), (1,)), ((), ())), preferred_element_type=F32
            )
        acc[...] = total

    def panel_rows(r):
        return pl.ds(pl.multiple_of(r * rows, rows), rows)

    def panel_copy(d):
        peer = ri_peer(d)
        return remote(acc.at[panel_rows(peer)], panels.at[ri], p_ss.at[d], p_rs.at[d], {"ri": peer})

    def send_panel(d, carry):
        panel_copy(d).start()
        return carry

    lax.fori_loop(1, n_ri, send_panel, 0)
    panels[ri] = acc[panel_rows(ri), :]

    def take_panel(d, carry):
        panel_copy(d).wait_recv()
        return carry

    lax.fori_loop(1, n_ri, take_panel, 0)
    own_x[x] = jnp.sum(panels[...], axis=0)
    x_copies = [remote(own_x.at[x], own_x.at[x], x_ss.at[d], x_rs.at[d], {"ao": x_peer(d)}) for d in range(1, n_x)]
    for copy in x_copies:
        copy.start()
    for copy in x_copies:
        copy.wait_recv()
    own_z[z] = jnp.sum(own_x[...], axis=0)
    z_copies = [remote(own_z.at[z], own_z.at[z], z_ss.at[d], z_rs.at[d], {"ao": z_peer(d)}) for d in range(1, n_z)]
    for copy in z_copies:
        copy.start()
    for copy in z_copies:
        copy.wait_recv()
    o_ref[...] = -jnp.sum(own_z[...], axis=0)

    to_right.wait_send()
    to_left.wait_send()
    for j in range(3):
        for copy in m_copies(j):
            copy.wait_send()
        drain(bt, b_all, b_ss, b_rs, j)
        drain(nt, n_all, n_ss, n_rs, j)

    def sent_panel(d, carry):
        panel_copy(d).wait_send()
        return carry

    lax.fori_loop(1, n_ri, sent_panel, 0)
    for copy in x_copies + z_copies:
        copy.wait_send()


def solution(mesh):
    n_ao, n_ri = mesh.shape["ao"], mesh.shape["ri"]
    n_z = 8
    n_x = n_ao // n_z

    def per_device(three_center, occ_band, virt_band, three_mask, occ_mask, virt_mask):
        rows = three_center.shape[0]
        tile = occ_band.shape[0]
        share = tile // n_ri
        size = n_ri * rows
        dma = pltpu.SemaphoreType.DMA
        vmem = pl.BlockSpec(memory_space=pltpu.VMEM)
        smem = pl.BlockSpec(memory_space=pltpu.SMEM)
        return pl.pallas_call(
            functools.partial(kernel, n_ao, n_ri, n_x, n_z, tile, rows),
            out_shape=jax.ShapeDtypeStruct((rows, size), F32),
            in_specs=[vmem, vmem, vmem, smem, smem, smem],
            out_specs=vmem,
            scratch_shapes=[
                pltpu.VMEM((rows * tile, tile), F32),
                pltpu.VMEM((3 * tile, rows, tile), BF16),
                pltpu.VMEM((tile, 5 * tile), BF16),
                pltpu.VMEM((tile, 4 * tile), BF16),
                pltpu.VMEM((tile, 4 * tile), BF16),
                pltpu.VMEM((5 * tile, 3 * tile), BF16),
                pltpu.VMEM((tile, 3 * tile), BF16),
                pltpu.VMEM((rows, 5 * tile, tile), BF16),
                pltpu.VMEM((rows, 3 * tile, tile), BF16),
                pltpu.VMEM((rows, 3 * tile, tile), BF16),
                pltpu.VMEM((3 * tile, rows, tile), BF16),
                pltpu.VMEM((3, n_ri, share, rows, tile), BF16),
                pltpu.VMEM((3, n_ri, share, rows, tile), BF16),
                pltpu.VMEM((size, size), F32),
                pltpu.VMEM((n_ri, rows, size), F32),
                pltpu.VMEM((n_x, rows, size), F32),
                pltpu.VMEM((n_z, rows, size), F32),
                dma((2,)), dma((2,)),
                dma((2, 3)), dma((2, 3)),
                dma((3, n_ri)), dma((3, n_ri)),
                dma((3, n_ri)), dma((3, n_ri)),
                dma((n_ri,)), dma((n_ri,)),
                dma((n_x,)), dma((n_x,)),
                dma((n_z,)), dma((n_z,)),
            ],
            compiler_params=pltpu.CompilerParams(
                collective_id=0, has_side_effects=True, vmem_limit_bytes=48 * 1024 * 1024
            ),
        )(three_center, occ_band, virt_band, three_mask, occ_mask, virt_mask)

    return jax.shard_map(
        per_device,
        mesh=mesh,
        in_specs=(P("ri", "ao", None), P("ao", None), P("ao", None), P("ao", None), P("ao", None), P("ao", None)),
        out_specs=P("ri", None),
        check_vma=False,
    )
```

time: 354 us -> 113 us (0.32)
  the two profiles are of different devices: /device:TPU:32 before, /device:TPU:1 now
where the time goes in v1:
time: 113 us
  Pallas kernels  107 us (95%)
  local copies, waits for them, and re-layouts  5.79 us (5%)
    pallas_call x1, Pallas kernels, per_device(): pl.pallas_call(functools.partial(kernel, n_ao, n_ri, n_x, n_z, tile, rows...  107 us
    unnamed x13, local copies, waits for them, and re-layouts  5.79 us

profile of v1, /device:TPU:1, one launch (start us, length us, event | category | flops | bytes accessed | tf_op | source)
XLA Modules:
  0.0 113.0 jit_solution(652318700217642762)
XLA Ops:
  0.0 0.0 copy-start
  0.0 1.4 %copy-done = bf16[16,384,128]{2,1,0:T(8,128)(2,1)S(1)} copy-done((bf16[16,384,128]{2,1,0:T(8,128)(2,1)S(1)}, bf16[16,384,128]{2,1,0:T(8,128)(2,1)}, u32[]{:S(2)}) %copy-start) | copy-done | bytes 1572888
  1.4 0.0 copy-start.1
  1.4 0.9 copy-done.1
  2.3 0.0 copy-start.2
  2.3 0.9 copy-done.2
  3.2 0.0 copy-start.3
  3.2 0.7 copy-done.3
  3.9 0.0 copy-start.4
  3.9 0.7 copy-done.4
  4.5 0.0 copy-start.5
  4.5 0.7 copy-done.5
  5.2 107.2 %shard_map.64 = f32[16,256]{1,0:T(8,128)S(1)} custom-call(bf16[16,384,128]{2,1,0:T(8,128)(2,1)S(1)} %copy-done, bf16[128,640]{1,0:T(8,128)(2,1)S(1)} %copy-done.1, bf16[128,384]{1,0:T(8,128)(2,1)S(1)} %copy-done.2, s32[1,3]{1,0:T(1,128)S(1)} %copy-done.3, s32[1,5]{1,0:T(1,128)S(1)} %copy-done.4, s32[1,3]{1,0:T(1,128)S(1)} %copy-done.5), custom_call_target="tpu_custom_call" | custom-call | tf_op jit(solution)/shard_map/pallas_call | solution.py:278
  112.4 0.6 copy.8
Async XLA Ops:
  0.0 1.4 %copy-start = (bf16[16,384,128]{2,1,0:T(8,128)(2,1)S(1)}, bf16[16,384,128]{2,1,0:T(8,128)(2,1)}, u32[]{:S(2)}) copy-start(bf16[16,384,128]{2,1,0:T(8,128)(2,1)} %b_ref.1) | copy-start | bytes 4718596
  1.4 0.9 copy-start.1
  2.3 0.9 copy-start.2
  3.2 0.7 copy-start.3
  3.9 0.7 copy-start.4
  4.5 0.7 copy-start.5

commit v2 on v1

--- a/solution.py
+++ b/solution.py
@@ -14,16 +14,26 @@
 
 def kernel(
     n_ao, n_ri, n_x, n_z, tile, rows,
-    b_ref, occ_ref, virt_ref, tm_ref, om_ref, vm_ref, o_ref,
+    b_hbm, occ_hbm, virt_hbm, tm_hbm, om_hbm, vm_hbm, o_ref,
+    b_ref, occ_ref, virt_ref, tm_ref, om_ref, vm_ref,
     wide, bt, occ_own, occ_left, occ_right, green, virt, m_buf, m_left, m_right,
     nt, b_all, n_all, acc, panels, own_x, own_z,
-    occ_ss, occ_rs, m_ss, m_rs, b_ss, b_rs, n_ss, n_rs, p_ss, p_rs, x_ss, x_rs, z_ss, z_rs,
+    in_sem, occ_ss, occ_rs, m_ss, m_rs, b_ss, b_rs, f_ss, f_rs, n_ss, n_rs, p_ss, p_rs, x_ss, x_rs, z_ss, z_rs,
 ):
     ao = lax.axis_index("ao")
     ri = lax.axis_index("ri")
     x, z = ao // n_z, lax.rem(ao, n_z)
+    y, core = ri // 2, lax.rem(ri, 2)
+    n_y = n_ri // 2
+    half = n_ri // 2
+    side = ri // half
     right, left = lax.rem(ao + 1, n_ao), lax.rem(ao + n_ao - 1, n_ao)
     share = tile // n_ri
+    wider = 2 * share
+
+    def far_first(i):
+        step = (i + 1) // 2
+        return n_y // 2 + step - 2 * step * lax.rem(i, 2)
 
     def remote(src, dst, ss, rs, where):
         return pltpu.make_async_remote_copy(
@@ -38,6 +48,24 @@
 
     def z_peer(d):
         return x * n_z + lax.rem(z + d, n_z)
+
+    b_in = [
+        pltpu.make_async_copy(
+            b_hbm.at[:, pl.ds(j * tile, tile), :], b_ref.at[:, pl.ds(j * tile, tile), :], in_sem.at[j]
+        )
+        for j in range(3)
+    ]
+    small_in = [
+        pltpu.make_async_copy(source, target, in_sem.at[3 + i])
+        for i, (source, target) in enumerate(
+            ((tm_hbm, tm_ref), (om_hbm, om_ref), (vm_hbm, vm_ref), (occ_hbm, occ_ref), (virt_hbm, virt_ref))
+        )
+    ]
+    b_in[0].start()
+    for copy in small_in:
+        copy.start()
+    b_in[1].start()
+    b_in[2].start()
 
     barrier = pltpu.get_barrier_semaphore()
 
@@ -57,6 +85,8 @@
     for d in range(1, n_x):
         greet({"ao": x_peer(d)})
 
+    for copy in small_in:
+        copy.wait()
     for j in range(5):
         cols = pl.ds(j * tile, tile)
         occ_own[:, cols] = (occ_ref[:, cols].astype(F32) * om_ref[0, j].astype(F32)).astype(BF16)
@@ -82,6 +112,7 @@
 
         lax.fori_loop(0, rows, body, 0)
 
+    b_in[0].wait()
     widen_b(0)
     regroup(wide, tile, bt, 0)
 
@@ -92,39 +123,101 @@
     to_right.start()
     to_left.start()
 
-    def share_copy(source, target, ss, rs, j, d):
-        peer = ri_peer(d)
+    def b_copy(j, i):
+        peer = lax.rem(y + far_first(i // 2), n_y) * 2 + lax.rem(core + 1 + i, 2)
         return remote(
-            source.at[pl.ds(pl.multiple_of(j * tile + peer * share, share), share)],
-            target.at[j, ri],
-            ss.at[j, d],
-            rs.at[j, d],
+            bt.at[pl.ds(pl.multiple_of(j * tile + peer * share, share), share)],
+            b_all.at[j, core_of(peer), ri],
+            b_ss.at[j, i],
+            b_rs.at[j, ri],
             {"ri": peer},
         )
 
-    def spread(source, target, ss, rs, j):
+    def core_of(peer):
+        return lax.rem(peer, 2)
+
+    def spread_b(j):
+        def body(i, carry):
+            b_copy(j, i).start()
+            return carry
+
+        lax.fori_loop(0, n_ri - 1, body, 0)
+        b_all[j, core, ri] = bt[pl.ds(pl.multiple_of(j * tile + ri * share, share), share)]
+
+    def b_arrive(j):
         def body(d, carry):
-            share_copy(source, target, ss, rs, j, d).start()
+            source = ri_peer(d)
+            remote(
+                bt.at[pl.ds(0, share)], b_all.at[j, core, source], b_ss.at[j, 0], b_rs.at[j, source], {"ri": source}
+            ).wait_recv()
             return carry
 
         lax.fori_loop(1, n_ri, body, 0)
-        target[j, ri] = source[pl.ds(pl.multiple_of(j * tile + ri * share, share), share)]
-
-    def arrive(source, target, ss, rs, j):
-        def body(d, carry):
-            share_copy(source, target, ss, rs, j, d).wait_recv()
-            return carry
-
-        lax.fori_loop(1, n_ri, body, 0)
-
-    def drain(source, target, ss, rs, j):
-        def body(d, carry):
-            share_copy(source, target, ss, rs, j, d).wait_send()
-            return carry
-
-        lax.fori_loop(1, n_ri, body, 0)
-
-    spread(bt, b_all, b_ss, b_rs, 0)
+
+    def b_drain(j):
+        def body(i, carry):
+            b_copy(j, i).wait_send()
+            return carry
+
+        lax.fori_loop(0, n_ri - 1, body, 0)
+
+    def forward(j):
+        return remote(b_all.at[j, core], b_all.at[j, core], f_ss.at[j], f_rs.at[j], {"ri": y * 2 + 1 - core})
+
+    def forwarded(j):
+        return remote(b_all.at[j, 1 - core], b_all.at[j, 1 - core], f_ss.at[j], f_rs.at[j], {"ri": y * 2 + 1 - core})
+
+    def n_copy(j, i):
+        chip = lax.rem(y + far_first(i), n_y)
+        return remote(
+            nt.at[pl.ds(pl.multiple_of(j * tile + chip * wider, wider), wider)],
+            n_all.at[j, lax.rem(ri, half)],
+            n_ss.at[j, i],
+            n_rs.at[j, lax.rem(ri, half)],
+            {"ri": chip * 2 + side},
+        )
+
+    def spread_n(j):
+        def body(i, carry):
+            n_copy(j, i).start()
+            return carry
+
+        lax.fori_loop(0, n_y - 1, body, 0)
+
+        @pl.when(core != side)
+        def _():
+            n_copy(j, n_y - 1).start()
+
+        @pl.when(core == side)
+        def _():
+            n_all[j, lax.rem(ri, half)] = nt[pl.ds(pl.multiple_of(j * tile + y * wider, wider), wider)]
+
+    def n_drain(j):
+        def body(i, carry):
+            n_copy(j, i).wait_send()
+            return carry
+
+        lax.fori_loop(0, n_y - 1, body, 0)
+
+        @pl.when(core != side)
+        def _():
+            n_copy(j, n_y - 1).wait_send()
+
+    def n_arrive(j, s):
+        source = core * half + s
+
+        @pl.when(source != ri)
+        def _():
+            remote(
+                nt.at[pl.ds(0, wider)], n_all.at[j, s], n_ss.at[j, 0], n_rs.at[j, s], {"ri": source}
+            ).wait_recv()
+
+    spread_b(0)
+    for j in (1, 2):
+        b_in[j].wait()
+        widen_b(j)
+        regroup(wide, tile, bt, j * tile)
+        spread_b(j)
 
     to_right.wait_recv()
     to_left.wait_recv()
@@ -166,11 +259,6 @@
     make_m(4, 1)
     for copy in m_copies(2):
         copy.start()
-
-    for j in (1, 2):
-        widen_b(j)
-        regroup(wide, tile, bt, j * tile)
-        spread(bt, b_all, b_ss, b_rs, j)
 
     for j in range(3):
         for copy in m_copies(j):
@@ -192,45 +280,88 @@
 
         lax.fori_loop(0, rows, n_body, 0)
         regroup(wide, tile, nt, j * tile)
-        spread(nt, n_all, n_ss, n_rs, j)
-
-    acc[...] = jnp.zeros_like(acc)
+        spread_n(j)
+        b_arrive(j)
+        forward(j).start()
+
+    def chi_part(j, first, count):
+        size = count * rows
+        total = None
+        for l in range(0, wider, 2):
+            which, at = l // share, l % share
+            lhs = jnp.concatenate(
+                [n_all[j, pl.ds(first, count), l + k].reshape(size, tile) for k in (0, 1)], axis=1
+            )
+            rhs = jnp.concatenate(
+                [b_all[j, which, :, at + k].reshape(n_ri * rows, tile) for k in (0, 1)], axis=1
+            )
+            part = lax.dot_general(lhs, rhs, (((1,), (1,)), ((), ())), preferred_element_type=F32)
+            total = part if total is None else total + part
+        return total
+
+    for j in range(2):
+        forwarded(j).wait_recv()
+
+        def n_wait(s, carry, j=j):
+            n_arrive(j, s)
+            return carry
+
+        lax.fori_loop(0, half, n_wait, 0)
+        acc[...] = chi_part(j, 0, half) if j == 0 else acc[...] + chi_part(j, 0, half)
+    forwarded(2).wait_recv()
+    to_right.wait_send()
+    to_left.wait_send()
     for j in range(3):
-        arrive(bt, b_all, b_ss, b_rs, j)
-        arrive(nt, n_all, n_ss, n_rs, j)
-        total = acc[...]
-        for l in range(0, share, 2):
-            size = n_ri * rows
-
-            def pair_of(ref):
-                return jnp.concatenate(
-                    [ref[j, :, l].reshape(size, tile), ref[j, :, l + 1].reshape(size, tile)], axis=1
-                )
-
-            total = total + lax.dot_general(
-                pair_of(n_all), pair_of(b_all), (((1,), (1,)), ((), ())), preferred_element_type=F32
-            )
-        acc[...] = total
-
-    def panel_rows(r):
-        return pl.ds(pl.multiple_of(r * rows, rows), rows)
-
-    def panel_copy(d):
-        peer = ri_peer(d)
-        return remote(acc.at[panel_rows(peer)], panels.at[ri], p_ss.at[d], p_rs.at[d], {"ri": peer})
-
-    def send_panel(d, carry):
-        panel_copy(d).start()
+        for copy in m_copies(j):
+            copy.wait_send()
+        b_drain(j)
+        forward(j).wait_send()
+
+    def panel_copy(s):
+        return remote(
+            acc.at[pl.ds(pl.multiple_of(s * rows, rows), rows)],
+            panels.at[y],
+            p_ss.at[s],
+            p_rs.at[y],
+            {"ri": core * half + s},
+        )
+
+    def last(i, carry):
+        chip = lax.rem(y + far_first(i), n_y)
+
+        @pl.when(chip // (n_y // 2) == core)
+        def _():
+            s0 = 2 * lax.rem(chip, n_y // 2)
+            n_arrive(2, s0)
+            n_arrive(2, s0 + 1)
+            at = pl.ds(pl.multiple_of(s0 * rows, 2 * rows), 2 * rows)
+            acc[at, :] = acc[at, :] + chi_part(2, s0, 2)
+            for s in (s0, s0 + 1):
+
+                @pl.when(core * half + s != ri)
+                def _(s=s):
+                    panel_copy(s).start()
+
         return carry
 
-    lax.fori_loop(1, n_ri, send_panel, 0)
-    panels[ri] = acc[panel_rows(ri), :]
-
-    def take_panel(d, carry):
-        panel_copy(d).wait_recv()
+    lax.fori_loop(0, n_y, last, 0)
+
+    @pl.when(core == side)
+    def _():
+        panels[y] = acc[pl.ds(pl.multiple_of(lax.rem(ri, half) * rows, rows), rows), :]
+
+    for j in range(3):
+        n_drain(j)
+    def take_panel(chip, carry):
+        source = chip * 2 + side
+
+        @pl.when(source != ri)
+        def _():
+            remote(acc.at[pl.ds(0, rows)], panels.at[chip], p_ss.at[0], p_rs.at[chip], {"ri": source}).wait_recv()
+
         return carry
 
-    lax.fori_loop(1, n_ri, take_panel, 0)
+    lax.fori_loop(0, n_y, take_panel, 0)
     own_x[x] = jnp.sum(panels[...], axis=0)
     x_copies = [remote(own_x.at[x], own_x.at[x], x_ss.at[d], x_rs.at[d], {"ao": x_peer(d)}) for d in range(1, n_x)]
     for copy in x_copies:
@@ -245,19 +376,14 @@
         copy.wait_recv()
     o_ref[...] = -jnp.sum(own_z[...], axis=0)
 
-    to_right.wait_send()
-    to_left.wait_send()
-    for j in range(3):
-        for copy in m_copies(j):
-            copy.wait_send()
-        drain(bt, b_all, b_ss, b_rs, j)
-        drain(nt, n_all, n_ss, n_rs, j)
-
-    def sent_panel(d, carry):
-        panel_copy(d).wait_send()
+    def sent_panel(s, carry):
+        @pl.when(core * half + s != ri)
+        def _():
+            panel_copy(s).wait_send()
+
         return carry
 
-    lax.fori_loop(1, n_ri, sent_panel, 0)
+    lax.fori_loop(0, half, sent_panel, 0)
     for copy in x_copies + z_copies:
         copy.wait_send()
 
@@ -274,13 +400,18 @@
         size = n_ri * rows
         dma = pltpu.SemaphoreType.DMA
         vmem = pl.BlockSpec(memory_space=pltpu.VMEM)
-        smem = pl.BlockSpec(memory_space=pltpu.SMEM)
         return pl.pallas_call(
             functools.partial(kernel, n_ao, n_ri, n_x, n_z, tile, rows),
             out_shape=jax.ShapeDtypeStruct((rows, size), F32),
-            in_specs=[vmem, vmem, vmem, smem, smem, smem],
+            in_specs=[pl.BlockSpec(memory_space=pl.ANY)] * 6,
             out_specs=vmem,
             scratch_shapes=[
+                pltpu.VMEM((rows, 3 * tile, tile), BF16),
+                pltpu.VMEM((tile, 5 * tile), BF16),
+                pltpu.VMEM((tile, 3 * tile), BF16),
+                pltpu.SMEM((1, 3), jnp.int32),
+                pltpu.SMEM((1, 5), jnp.int32),
+                pltpu.SMEM((1, 3), jnp.int32),
                 pltpu.VMEM((rows * tile, tile), F32),
                 pltpu.VMEM((3 * tile, rows, tile), BF16),
                 pltpu.VMEM((tile, 5 * tile), BF16),
@@ -292,23 +423,23 @@
                 pltpu.VMEM((rows, 3 * tile, tile), BF16),
                 pltpu.VMEM((rows, 3 * tile, tile), BF16),
                 pltpu.VMEM((3 * tile, rows, tile), BF16),
-                pltpu.VMEM((3, n_ri, share, rows, tile), BF16),
-                pltpu.VMEM((3, n_ri, share, rows, tile), BF16),
-                pltpu.VMEM((size, size), F32),
-                pltpu.VMEM((n_ri, rows, size), F32),
+                pltpu.VMEM((3, 2, n_ri, share, rows, tile), BF16),
+                pltpu.VMEM((3, n_ri // 2, 2 * share, rows, tile), BF16),
+                pltpu.VMEM((size // 2, size), F32),
+                pltpu.VMEM((n_ri // 2, rows, size), F32),
                 pltpu.VMEM((n_x, rows, size), F32),
                 pltpu.VMEM((n_z, rows, size), F32),
+                dma((8,)),
                 dma((2,)), dma((2,)),
                 dma((2, 3)), dma((2, 3)),
                 dma((3, n_ri)), dma((3, n_ri)),
-                dma((3, n_ri)), dma((3, n_ri)),
-                dma((n_ri,)), dma((n_ri,)),
+                dma((3,)), dma((3,)),
+                dma((3, n_ri // 2)), dma((3, n_ri // 2)),
+                dma((n_ri // 2,)), dma((n_ri // 2,)),
                 dma((n_x,)), dma((n_x,)),
                 dma((n_z,)), dma((n_z,)),
             ],
-            compiler_params=pltpu.CompilerParams(
-                collective_id=0, has_side_effects=True, vmem_limit_bytes=48 * 1024 * 1024
-            ),
+            compiler_params=pltpu.CompilerParams(collective_id=0, has_side_effects=True),
         )(three_center, occ_band, virt_band, three_mask, occ_mask, virt_mask)
 
     return jax.shard_map(

time: 113 us -> 102 us (0.903)
  Pallas kernels: 107 us -> 100 us
  local copies, waits for them, and re-layouts: 5.79 us -> 1.32 us
    pallas_call x1, Pallas kernels: 107 us -> 100 us  [per_device(): pl.pallas_call(functools.partial(kernel, n_ao, n_ri, n_x, n_z, tile, rows...]
    unnamed x13 -> x1, local copies, waits for them, and re-layouts: 5.79 us -> 1.32 us
where the time goes in v2:
time: 102 us
  Pallas kernels  100 us (98%)
  local copies, waits for them, and re-layouts  1.32 us (1%)
    pallas_call x1, Pallas kernels, per_device(): pl.pallas_call(functools.partial(kernel, n_ao, n_ri, n_x, n_z, tile, rows...  100 us

profile of v2, /device:TPU:1, one launch (start us, length us, event | category | flops | bytes accessed | tf_op | source)
XLA Modules:
  0.0 101.7 jit_solution(1619617574578725332)
XLA Ops:
  0.0 100.4 %shard_map.64 = f32[16,256]{1,0:T(8,128)} custom-call(bf16[16,384,128]{2,1,0:T(8,128)(2,1)} %b_hbm.1, bf16[128,640]{1,0:T(8,128)(2,1)} %occ_hbm.1, bf16[128,384]{1,0:T(8,128)(2,1)} %virt_hbm.1, s32[1,3]{1,0:T(1,128)} %tm_hbm.1, s32[1,5]{1,0:T(1,128)} %om_hbm.1, s32[1,3]{1,0:T(1,128)} %vm_hbm.1), custom_call_target="tpu_custom_call" | custom-call | tf_op jit(solution)/shard_map/pallas_call | solution.py:403
  100.4 1.3 %copy.8 = f32[16,256]{1,0:T(8,128)} copy(f32[16,256]{1,0:T(8,128)} %shard_map.64) | data formatting | bytes 32768

commit v3 on v2

--- a/solution.py
+++ b/solution.py
@@ -72,14 +72,13 @@
     def greet(where):
         pl.semaphore_signal(barrier, inc=1, device_id=where, device_id_type=MESH)
 
+    def greet_ri(i, carry):
+        greet({"ri": lax.rem(y + far_first(i // 2), n_y) * 2 + lax.rem(core + 1 + i, 2)})
+        return carry
+
+    lax.fori_loop(0, n_ri - 1, greet_ri, 0)
     greet({"ao": right})
     greet({"ao": left})
-
-    def greet_ri(d, carry):
-        greet({"ri": ri_peer(d)})
-        return carry
-
-    lax.fori_loop(1, n_ri, greet_ri, 0)
     for d in range(1, n_z):
         greet({"ao": z_peer(d)})
     for d in range(1, n_x):
@@ -128,8 +127,8 @@
         return remote(
             bt.at[pl.ds(pl.multiple_of(j * tile + peer * share, share), share)],
             b_all.at[j, core_of(peer), ri],
-            b_ss.at[j, i],
-            b_rs.at[j, ri],
+            b_ss.at[j],
+            b_rs.at[j],
             {"ri": peer},
         )
 
@@ -144,22 +143,9 @@
         lax.fori_loop(0, n_ri - 1, body, 0)
         b_all[j, core, ri] = bt[pl.ds(pl.multiple_of(j * tile + ri * share, share), share)]
 
-    def b_arrive(j):
-        def body(d, carry):
-            source = ri_peer(d)
-            remote(
-                bt.at[pl.ds(0, share)], b_all.at[j, core, source], b_ss.at[j, 0], b_rs.at[j, source], {"ri": source}
-            ).wait_recv()
-            return carry
-
-        lax.fori_loop(1, n_ri, body, 0)
-
-    def b_drain(j):
-        def body(i, carry):
-            b_copy(j, i).wait_send()
-            return carry
-
-        lax.fori_loop(0, n_ri - 1, body, 0)
+    def b_all_of(j):
+        rest = bt.at[pl.ds(0, (n_ri - 1) * share)]
+        return remote(rest, rest, b_ss.at[j], b_rs.at[j], {"ri": y * 2 + 1 - core})
 
     def forward(j):
         return remote(b_all.at[j, core], b_all.at[j, core], f_ss.at[j], f_rs.at[j], {"ri": y * 2 + 1 - core})
@@ -172,8 +158,8 @@
         return remote(
             nt.at[pl.ds(pl.multiple_of(j * tile + chip * wider, wider), wider)],
             n_all.at[j, lax.rem(ri, half)],
-            n_ss.at[j, i],
-            n_rs.at[j, lax.rem(ri, half)],
+            n_ss.at[j],
+            n_rs.at[j if j < 2 else 2 + lax.rem(ri, half) // 2],
             {"ri": chip * 2 + side},
         )
 
@@ -192,25 +178,27 @@
         def _():
             n_all[j, lax.rem(ri, half)] = nt[pl.ds(pl.multiple_of(j * tile + y * wider, wider), wider)]
 
+    def n_of(sources, sem, ss):
+        some = nt.at[pl.ds(0, sources * wider)]
+        return remote(some, some, ss, n_rs.at[sem], {"ri": y * 2 + 1 - core})
+
     def n_drain(j):
-        def body(i, carry):
-            n_copy(j, i).wait_send()
-            return carry
-
-        lax.fori_loop(0, n_y - 1, body, 0)
-
         @pl.when(core != side)
         def _():
-            n_copy(j, n_y - 1).wait_send()
-
-    def n_arrive(j, s):
-        source = core * half + s
-
-        @pl.when(source != ri)
-        def _():
-            remote(
-                nt.at[pl.ds(0, wider)], n_all.at[j, s], n_ss.at[j, 0], n_rs.at[j, s], {"ri": source}
-            ).wait_recv()
+            n_of(n_y, 0, n_ss.at[j]).wait_send()
+
+        @pl.when(core == side)
+        def _():
+            n_of(n_y - 1, 0, n_ss.at[j]).wait_send()
+
+    def n_arrive(j):
+        @pl.when(core != side)
+        def _():
+            n_of(half, j, n_ss.at[j]).wait_recv()
+
+        @pl.when(core == side)
+        def _():
+            n_of(half - 1, j, n_ss.at[j]).wait_recv()
 
     spread_b(0)
     for j in (1, 2):
@@ -246,9 +234,13 @@
     def m_copies(j):
         cols = pl.ds(j * tile, tile)
         return (
-            remote(m_buf.at[:, pl.ds((j + 2) * tile, tile), :], m_left.at[:, cols, :], m_ss.at[0, j], m_rs.at[0, j], {"ao": right}),
-            remote(m_buf.at[:, cols, :], m_right.at[:, cols, :], m_ss.at[1, j], m_rs.at[1, j], {"ao": left}),
-        )
+            remote(m_buf.at[:, pl.ds((j + 2) * tile, tile), :], m_left.at[:, cols, :], m_ss.at[j], m_rs.at[j], {"ao": right}),
+            remote(m_buf.at[:, cols, :], m_right.at[:, cols, :], m_ss.at[j], m_rs.at[j], {"ao": left}),
+        )
+
+    def m_both(j):
+        both = m_left.at[:, pl.ds(0, 2 * tile), :]
+        return remote(both, both, m_ss.at[j], m_rs.at[j], {"ao": right})
 
     make_m(0, 3)
     for copy in m_copies(0):
@@ -261,8 +253,7 @@
         copy.start()
 
     for j in range(3):
-        for copy in m_copies(j):
-            copy.wait_recv()
+        m_both(j).wait_recv()
 
         def n_body(p, carry, j=j):
             needed = jnp.concatenate(
@@ -281,7 +272,7 @@
         lax.fori_loop(0, rows, n_body, 0)
         regroup(wide, tile, nt, j * tile)
         spread_n(j)
-        b_arrive(j)
+        b_all_of(j).wait_recv()
         forward(j).start()
 
     def chi_part(j, first, count):
@@ -302,27 +293,22 @@
     for j in range(2):
         forwarded(j).wait_recv()
 
-        def n_wait(s, carry, j=j):
-            n_arrive(j, s)
-            return carry
-
-        lax.fori_loop(0, half, n_wait, 0)
+        n_arrive(j)
         acc[...] = chi_part(j, 0, half) if j == 0 else acc[...] + chi_part(j, 0, half)
     forwarded(2).wait_recv()
     to_right.wait_send()
     to_left.wait_send()
     for j in range(3):
-        for copy in m_copies(j):
-            copy.wait_send()
-        b_drain(j)
+        m_both(j).wait_send()
+        b_all_of(j).wait_send()
         forward(j).wait_send()
 
     def panel_copy(s):
         return remote(
             acc.at[pl.ds(pl.multiple_of(s * rows, rows), rows)],
             panels.at[y],
-            p_ss.at[s],
-            p_rs.at[y],
+            p_ss,
+            p_rs,
             {"ri": core * half + s},
         )
 
@@ -332,8 +318,15 @@
         @pl.when(chip // (n_y // 2) == core)
         def _():
             s0 = 2 * lax.rem(chip, n_y // 2)
-            n_arrive(2, s0)
-            n_arrive(2, s0 + 1)
+
+            @pl.when(chip != y)
+            def _():
+                n_of(2, 2 + s0 // 2, n_ss.at[2]).wait_recv()
+
+            @pl.when(chip == y)
+            def _():
+                n_of(1, 2 + s0 // 2, n_ss.at[2]).wait_recv()
+
             at = pl.ds(pl.multiple_of(s0 * rows, 2 * rows), 2 * rows)
             acc[at, :] = acc[at, :] + chi_part(2, s0, 2)
             for s in (s0, s0 + 1):
@@ -352,40 +345,46 @@
 
     for j in range(3):
         n_drain(j)
-    def take_panel(chip, carry):
-        source = chip * 2 + side
-
-        @pl.when(source != ri)
-        def _():
-            remote(acc.at[pl.ds(0, rows)], panels.at[chip], p_ss.at[0], p_rs.at[chip], {"ri": source}).wait_recv()
-
-        return carry
-
-    lax.fori_loop(0, n_y, take_panel, 0)
+    def panels_of(count):
+        some = acc.at[pl.ds(0, count * rows)]
+        return remote(some, some, p_ss, p_rs, {"ri": y * 2 + 1 - core})
+
+    @pl.when(core != side)
+    def _():
+        panels_of(n_y).wait_recv()
+
+    @pl.when(core == side)
+    def _():
+        panels_of(n_y - 1).wait_recv()
+
     own_x[x] = jnp.sum(panels[...], axis=0)
-    x_copies = [remote(own_x.at[x], own_x.at[x], x_ss.at[d], x_rs.at[d], {"ao": x_peer(d)}) for d in range(1, n_x)]
-    for copy in x_copies:
-        copy.start()
-    for copy in x_copies:
-        copy.wait_recv()
+    for d in range(1, n_x):
+        remote(own_x.at[x], own_x.at[x], x_ss, x_rs, {"ao": x_peer(d)}).start()
+
+    def rest_of(ref, count, ss, rs, where):
+        return remote(ref.at[pl.ds(0, count)], ref.at[pl.ds(0, count)], ss, rs, where)
+
+    if n_x > 1:
+        x_rest = rest_of(own_x, n_x - 1, x_ss, x_rs, {"ao": x_peer(1)})
+        x_rest.wait_recv()
     own_z[z] = jnp.sum(own_x[...], axis=0)
-    z_copies = [remote(own_z.at[z], own_z.at[z], z_ss.at[d], z_rs.at[d], {"ao": z_peer(d)}) for d in range(1, n_z)]
-    for copy in z_copies:
-        copy.start()
-    for copy in z_copies:
-        copy.wait_recv()
+    for d in range(1, n_z):
+        remote(own_z.at[z], own_z.at[z], z_ss, z_rs, {"ao": z_peer(d)}).start()
+    z_rest = rest_of(own_z, n_z - 1, z_ss, z_rs, {"ao": z_peer(1)})
+    z_rest.wait_recv()
     o_ref[...] = -jnp.sum(own_z[...], axis=0)
 
-    def sent_panel(s, carry):
-        @pl.when(core * half + s != ri)
-        def _():
-            panel_copy(s).wait_send()
-
-        return carry
-
-    lax.fori_loop(0, half, sent_panel, 0)
-    for copy in x_copies + z_copies:
-        copy.wait_send()
+    @pl.when(core != side)
+    def _():
+        panels_of(half).wait_send()
+
+    @pl.when(core == side)
+    def _():
+        panels_of(half - 1).wait_send()
+
+    if n_x > 1:
+        x_rest.wait_send()
+    z_rest.wait_send()
 
 
 def solution(mesh):
@@ -402,7 +401,7 @@
         vmem = pl.BlockSpec(memory_space=pltpu.VMEM)
         return pl.pallas_call(
             functools.partial(kernel, n_ao, n_ri, n_x, n_z, tile, rows),
-            out_shape=jax.ShapeDtypeStruct((rows, size), F32),
+            out_shape=pltpu.VMEM((rows, size), F32),
             in_specs=[pl.BlockSpec(memory_space=pl.ANY)] * 6,
             out_specs=vmem,
             scratch_shapes=[
@@ -431,13 +430,11 @@
                 pltpu.VMEM((n_z, rows, size), F32),
                 dma((8,)),
                 dma((2,)), dma((2,)),
-                dma((2, 3)), dma((2, 3)),
-                dma((3, n_ri)), dma((3, n_ri)),
                 dma((3,)), dma((3,)),
-                dma((3, n_ri // 2)), dma((3, n_ri // 2)),
-                dma((n_ri // 2,)), dma((n_ri // 2,)),
-                dma((n_x,)), dma((n_x,)),
-                dma((n_z,)), dma((n_z,)),
+                dma((3,)), dma((3,)),
+                dma((3,)), dma((3,)),
+                dma((3,)), dma((2 + n_ri // 4,)),
+                dma, dma, dma, dma, dma, dma,
             ],
             compiler_params=pltpu.CompilerParams(collective_id=0, has_side_effects=True),
         )(three_center, occ_band, virt_band, three_mask, occ_mask, virt_mask)

time: 102 us -> 99.1 us (0.972)
  Pallas kernels: 100 us -> 98.3 us
    pallas_call x1, Pallas kernels: 100 us -> 98.3 us  [per_device(): pl.pallas_call(functools.partial(kernel, n_ao, n_ri, n_x, n_z, tile, rows...]
where the time goes in v3:
time: 99.1 us; the launch traced here: 99 us
  Pallas kernels  98.3 us (99%)
    pallas_call x1, Pallas kernels, per_device(): pl.pallas_call(functools.partial(kernel, n_ao, n_ri, n_x, n_z, tile, rows...  98.3 us

profile of v3, /device:TPU:1, one launch (start us, length us, event | category | flops | bytes accessed | tf_op | source)
XLA Modules:
  0.0 99.0 jit_solution(1437394164267535626)
XLA Ops:
  0.0 98.3 %shard_map.64 = f32[16,256]{1,0:T(8,128)S(1)} custom-call(bf16[16,384,128]{2,1,0:T(8,128)(2,1)} %b_hbm.1, bf16[128,640]{1,0:T(8,128)(2,1)} %occ_hbm.1, bf16[128,384]{1,0:T(8,128)(2,1)} %virt_hbm.1, s32[1,3]{1,0:T(1,128)} %tm_hbm.1, s32[1,5]{1,0:T(1,128)} %om_hbm.1, s32[1,3]{1,0:T(1,128)} %vm_hbm.1), custom_call_target="tpu_custom_call" | custom-call | tf_op jit(solution)/shard_map/pallas_call | solution.py:402
  98.3 0.6 copy.8

commit v4 on v3

--- a/solution.py
+++ b/solution.py
@@ -17,7 +17,7 @@
     b_hbm, occ_hbm, virt_hbm, tm_hbm, om_hbm, vm_hbm, o_ref,
     b_ref, occ_ref, virt_ref, tm_ref, om_ref, vm_ref,
     wide, bt, occ_own, occ_left, occ_right, green, virt, m_buf, m_left, m_right,
-    nt, b_all, n_all, acc, panels, own_x, own_z,
+    nt, b_all, n_all, acc, done, panels, own_x, own_z,
     in_sem, occ_ss, occ_rs, m_ss, m_rs, b_ss, b_rs, f_ss, f_rs, n_ss, n_rs, p_ss, p_rs, x_ss, x_rs, z_ss, z_rs,
 ):
     ao = lax.axis_index("ao")
@@ -84,15 +84,6 @@
     for d in range(1, n_x):
         greet({"ao": x_peer(d)})
 
-    for copy in small_in:
-        copy.wait()
-    for j in range(5):
-        cols = pl.ds(j * tile, tile)
-        occ_own[:, cols] = (occ_ref[:, cols].astype(F32) * om_ref[0, j].astype(F32)).astype(BF16)
-    for j in range(3):
-        cols = pl.ds(j * tile, tile)
-        virt[:, cols] = (virt_ref[:, cols].astype(F32) * vm_ref[0, j].astype(F32)).astype(BF16)
-
     def regroup(source_rows, stride, target, lam0):
         def body(l, carry):
             target[lam0 + l] = source_rows[pl.ds(l, rows, stride=stride), :].astype(BF16)
@@ -111,16 +102,13 @@
 
         lax.fori_loop(0, rows, body, 0)
 
+    small_in[0].wait()
     b_in[0].wait()
     widen_b(0)
     regroup(wide, tile, bt, 0)
 
     pl.semaphore_wait(barrier, 2 + n_ri - 1 + n_z - 1 + n_x - 1)
 
-    to_right = remote(occ_own.at[:, pl.ds(tile, 4 * tile)], occ_left, occ_ss.at[0], occ_rs.at[0], {"ao": right})
-    to_left = remote(occ_own.at[:, pl.ds(0, 4 * tile)], occ_right, occ_ss.at[1], occ_rs.at[1], {"ao": left})
-    to_right.start()
-    to_left.start()
 
     def b_copy(j, i):
         peer = lax.rem(y + far_first(i // 2), n_y) * 2 + lax.rem(core + 1 + i, 2)
@@ -201,6 +189,20 @@
             n_of(half - 1, j, n_ss.at[j]).wait_recv()
 
     spread_b(0)
+    for copy in small_in[1:]:
+        copy.wait()
+    for j in range(5):
+        cols = pl.ds(j * tile, tile)
+        occ_own[:, cols] = (occ_ref[:, cols].astype(F32) * om_ref[0, j].astype(F32)).astype(BF16)
+    for j in range(3):
+        cols = pl.ds(j * tile, tile)
+        virt[:, cols] = (virt_ref[:, cols].astype(F32) * vm_ref[0, j].astype(F32)).astype(BF16)
+
+    to_right = remote(occ_own.at[:, pl.ds(tile, 4 * tile)], occ_left, occ_ss.at[0], occ_rs.at[0], {"ao": right})
+    to_left = remote(occ_own.at[:, pl.ds(0, 4 * tile)], occ_right, occ_ss.at[1], occ_rs.at[1], {"ao": left})
+    to_right.start()
+    to_left.start()
+
     for j in (1, 2):
         b_in[j].wait()
         widen_b(j)
@@ -305,7 +307,7 @@
 
     def panel_copy(s):
         return remote(
-            acc.at[pl.ds(pl.multiple_of(s * rows, rows), rows)],
+            done.at[pl.ds(pl.multiple_of(s * rows, rows), rows)],
             panels.at[y],
             p_ss,
             p_rs,
@@ -328,7 +330,7 @@
                 n_of(1, 2 + s0 // 2, n_ss.at[2]).wait_recv()
 
             at = pl.ds(pl.multiple_of(s0 * rows, 2 * rows), 2 * rows)
-            acc[at, :] = acc[at, :] + chi_part(2, s0, 2)
+            done[at, :] = (acc[at, :] + chi_part(2, s0, 2)).astype(BF16)
             for s in (s0, s0 + 1):
 
                 @pl.when(core * half + s != ri)
@@ -341,12 +343,12 @@
 
     @pl.when(core == side)
     def _():
-        panels[y] = acc[pl.ds(pl.multiple_of(lax.rem(ri, half) * rows, rows), rows), :]
+        panels[y] = done[pl.ds(pl.multiple_of(lax.rem(ri, half) * rows, rows), rows), :]
 
     for j in range(3):
         n_drain(j)
     def panels_of(count):
-        some = acc.at[pl.ds(0, count * rows)]
+        some = done.at[pl.ds(0, count * rows)]
         return remote(some, some, p_ss, p_rs, {"ri": y * 2 + 1 - core})
 
     @pl.when(core != side)
@@ -357,7 +359,7 @@
     def _():
         panels_of(n_y - 1).wait_recv()
 
-    own_x[x] = jnp.sum(panels[...], axis=0)
+    own_x[x] = jnp.sum(panels[...].astype(F32), axis=0)
     for d in range(1, n_x):
         remote(own_x.at[x], own_x.at[x], x_ss, x_rs, {"ao": x_peer(d)}).start()
 
@@ -367,12 +369,14 @@
     if n_x > 1:
         x_rest = rest_of(own_x, n_x - 1, x_ss, x_rs, {"ao": x_peer(1)})
         x_rest.wait_recv()
-    own_z[z] = jnp.sum(own_x[...], axis=0)
-    for d in range(1, n_z):
-        remote(own_z.at[z], own_z.at[z], z_ss, z_rs, {"ao": z_peer(d)}).start()
+    own_z[z] = jnp.sum(own_x[...], axis=0).astype(BF16)
+    for i in range(n_z - 1):
+        step = (i + 1) // 2
+        far = n_z // 2 + (step if i % 2 == 0 else -step)
+        remote(own_z.at[z], own_z.at[z], z_ss, z_rs, {"ao": z_peer(far)}).start()
     z_rest = rest_of(own_z, n_z - 1, z_ss, z_rs, {"ao": z_peer(1)})
     z_rest.wait_recv()
-    o_ref[...] = -jnp.sum(own_z[...], axis=0)
+    o_ref[...] = -jnp.sum(own_z[...].astype(F32), axis=0)
 
     @pl.when(core != side)
     def _():
@@ -425,9 +429,10 @@
                 pltpu.VMEM((3, 2, n_ri, share, rows, tile), BF16),
                 pltpu.VMEM((3, n_ri // 2, 2 * share, rows, tile), BF16),
                 pltpu.VMEM((size // 2, size), F32),
-                pltpu.VMEM((n_ri // 2, rows, size), F32),
+                pltpu.VMEM((size // 2, size), BF16),
+                pltpu.VMEM((n_ri // 2, rows, size), BF16),
                 pltpu.VMEM((n_x, rows, size), F32),
-                pltpu.VMEM((n_z, rows, size), F32),
+                pltpu.VMEM((n_z, rows, size), BF16),
                 dma((8,)),
                 dma((2,)), dma((2,)),
                 dma((3,)), dma((3,)),

time: 99.1 us -> 98 us (0.989)
  Pallas kernels: 98.3 us -> 97.2 us
    pallas_call x1, Pallas kernels: 98.3 us -> 97.2 us  [per_device(): pl.pallas_call(functools.partial(kernel, n_ao, n_ri, n_x, n_z, tile, rows...]
where the time goes in v4:
time: 98 us; the launch traced here: 97.9 us
  Pallas kernels  97.2 us (99%)
    pallas_call x1, Pallas kernels, per_device(): pl.pallas_call(functools.partial(kernel, n_ao, n_ri, n_x, n_z, tile, rows...  97.2 us

profile of v4, /device:TPU:1, one launch (start us, length us, event | category | flops | bytes accessed | tf_op | source)
XLA Modules:
  0.0 97.9 jit_solution(11174624809501099891)
XLA Ops:
  0.0 97.2 %shard_map.64 = f32[16,256]{1,0:T(8,128)S(1)} custom-call(bf16[16,384,128]{2,1,0:T(8,128)(2,1)} %b_hbm.1, bf16[128,640]{1,0:T(8,128)(2,1)} %occ_hbm.1, bf16[128,384]{1,0:T(8,128)(2,1)} %virt_hbm.1, s32[1,3]{1,0:T(1,128)} %tm_hbm.1, s32[1,5]{1,0:T(1,128)} %om_hbm.1, s32[1,3]{1,0:T(1,128)} %vm_hbm.1), custom_call_target="tpu_custom_call" | custom-call | tf_op jit(solution)/shard_map/pallas_call | solution.py:406
  97.3 0.6 copy.8

commit v5 on v4

--- a/solution.py
+++ b/solution.py
@@ -18,7 +18,7 @@
     b_ref, occ_ref, virt_ref, tm_ref, om_ref, vm_ref,
     wide, bt, occ_own, occ_left, occ_right, green, virt, m_buf, m_left, m_right,
     nt, b_all, n_all, acc, done, panels, own_x, own_z,
-    in_sem, occ_ss, occ_rs, m_ss, m_rs, b_ss, b_rs, f_ss, f_rs, n_ss, n_rs, p_ss, p_rs, x_ss, x_rs, z_ss, z_rs,
+    in_sem, up, down, z_up, z_down, x_up, occ_ss, occ_rs, m_ss, m_rs, b_ss, b_rs, f_ss, f_rs, n_ss, n_rs, p_ss, p_rs, x_ss, x_rs, z_ss, z_rs,
 ):
     ao = lax.axis_index("ao")
     ri = lax.axis_index("ri")
@@ -72,17 +72,14 @@
     def greet(where):
         pl.semaphore_signal(barrier, inc=1, device_id=where, device_id_type=MESH)
 
-    def greet_ri(i, carry):
-        greet({"ri": lax.rem(y + far_first(i // 2), n_y) * 2 + lax.rem(core + 1 + i, 2)})
-        return carry
-
-    lax.fori_loop(0, n_ri - 1, greet_ri, 0)
-    greet({"ao": right})
-    greet({"ao": left})
-    for d in range(1, n_z):
-        greet({"ao": z_peer(d)})
-    for d in range(1, n_x):
-        greet({"ao": x_peer(d)})
+    above, below = lax.rem(y + 1, n_y), lax.rem(y + n_y - 1, n_y)
+    for chip in (above, below):
+        greet({"ri": chip * 2 + core})
+        greet({"ri": chip * 2 + 1 - core})
+    greet({"ri": y * 2 + 1 - core})
+    x_beside = (1, n_x - 1) if n_x > 1 else ()
+    for where in [right, left, z_peer(1), z_peer(n_z - 1)] + [x_peer(d) for d in x_beside]:
+        greet({"ao": where})
 
     def regroup(source_rows, stride, target, lam0):
         def body(l, carry):
@@ -107,7 +104,34 @@
     widen_b(0)
     regroup(wide, tile, bt, 0)
 
-    pl.semaphore_wait(barrier, 2 + n_ri - 1 + n_z - 1 + n_x - 1)
+    pl.semaphore_wait(barrier, 5 + 4 + len(x_beside))
+
+    def tell(step):
+        pl.semaphore_signal(up.at[step], inc=1, device_id={"ri": above * 2 + core}, device_id_type=MESH)
+        if step < 2:
+            pl.semaphore_signal(down.at[step], inc=1, device_id={"ri": below * 2 + core}, device_id_type=MESH)
+
+    def hear(step):
+        pl.semaphore_wait(up.at[step], 1)
+        if step < 2:
+            pl.semaphore_wait(down.at[step], 1)
+
+    def tell_ao(step):
+        pl.semaphore_signal(z_up.at[step], inc=1, device_id={"ao": z_peer(1)}, device_id_type=MESH)
+        if step < 2:
+            pl.semaphore_signal(z_down.at[step], inc=1, device_id={"ao": z_peer(n_z - 1)}, device_id_type=MESH)
+        if step == 0 and x_beside:
+            pl.semaphore_signal(x_up, inc=1, device_id={"ao": x_peer(1)}, device_id_type=MESH)
+
+    def hear_ao(step):
+        pl.semaphore_wait(z_up.at[step], 1)
+        if step < 2:
+            pl.semaphore_wait(z_down.at[step], 1)
+        if step == 0 and x_beside:
+            pl.semaphore_wait(x_up, 1)
+
+    tell(0)
+    tell_ao(0)
 
 
     def b_copy(j, i):
@@ -128,7 +152,11 @@
             b_copy(j, i).start()
             return carry
 
-        lax.fori_loop(0, n_ri - 1, body, 0)
+        lax.fori_loop(0, n_ri - 2, body, 0)
+        own_b(j)
+
+    def own_b(j):
+        b_copy(j, n_ri - 2).start()
         b_all[j, core, ri] = bt[pl.ds(pl.multiple_of(j * tile + ri * share, share), share)]
 
     def b_all_of(j):
@@ -188,7 +216,31 @@
         def _():
             n_of(half - 1, j, n_ss.at[j]).wait_recv()
 
-    spread_b(0)
+    def b_by(j, steps):
+        chip = lax.rem(y + steps + n_y, n_y)
+        for other in (0, 1):
+            peer = chip * 2 + (core if other == 0 else 1 - core)
+            remote(
+                bt.at[pl.ds(pl.multiple_of(j * tile + peer * share, share), share)],
+                b_all.at[j, core_of(peer), ri],
+                b_ss.at[j],
+                b_rs.at[j],
+                {"ri": peer},
+            ).start()
+
+    b_by(0, 1)
+    b_by(0, -1)
+    hear(0)
+    tell(1)
+    b_by(0, 2)
+    b_by(0, -2)
+    hear(1)
+    tell(2)
+    b_by(0, 3)
+    b_by(0, -3)
+    hear(2)
+    b_by(0, 4)
+    own_b(0)
     for copy in small_in[1:]:
         copy.wait()
     for j in range(5):
@@ -254,6 +306,8 @@
     for copy in m_copies(2):
         copy.start()
 
+    hear_ao(0)
+    tell_ao(1)
     for j in range(3):
         m_both(j).wait_recv()
 
@@ -276,6 +330,10 @@
         spread_n(j)
         b_all_of(j).wait_recv()
         forward(j).start()
+        if j < 2:
+            hear_ao(j + 1)
+        if j == 0:
+            tell_ao(2)
 
     def chi_part(j, first, count):
         size = count * rows
@@ -434,6 +492,11 @@
                 pltpu.VMEM((n_x, rows, size), F32),
                 pltpu.VMEM((n_z, rows, size), BF16),
                 dma((8,)),
+                pltpu.SemaphoreType.REGULAR((3,)),
+                pltpu.SemaphoreType.REGULAR((2,)),
+                pltpu.SemaphoreType.REGULAR((3,)),
+                pltpu.SemaphoreType.REGULAR((2,)),
+                pltpu.SemaphoreType.REGULAR,
                 dma((2,)), dma((2,)),
                 dma((3,)), dma((3,)),
                 dma((3,)), dma((3,)),

time: 98 us -> 95.4 us (0.973)
  Pallas kernels: 97.2 us -> 94.4 us
    pallas_call x1, Pallas kernels: 97.2 us -> 94.4 us  [per_device(): pl.pallas_call(functools.partial(kernel, n_ao, n_ri, n_x, n_z, tile, rows...]
where the time goes in v5:
time: 95.4 us; the launch traced here: 95 us
  Pallas kernels  94.4 us (99%)
    pallas_call x1, Pallas kernels, per_device(): pl.pallas_call(functools.partial(kernel, n_ao, n_ri, n_x, n_z, tile, rows...  94.4 us

profile of v5, /device:TPU:1, one launch (start us, length us, event | category | flops | bytes accessed | tf_op | source)
XLA Modules:
  0.0 95.0 jit_solution(947790052145558994)
XLA Ops:
  0.0 94.4 %shard_map.64 = f32[16,256]{1,0:T(8,128)S(1)} custom-call(bf16[16,384,128]{2,1,0:T(8,128)(2,1)} %b_hbm.1, bf16[128,640]{1,0:T(8,128)(2,1)} %occ_hbm.1, bf16[128,384]{1,0:T(8,128)(2,1)} %virt_hbm.1, s32[1,3]{1,0:T(1,128)} %tm_hbm.1, s32[1,5]{1,0:T(1,128)} %om_hbm.1, s32[1,3]{1,0:T(1,128)} %vm_hbm.1), custom_call_target="tpu_custom_call" | custom-call | tf_op jit(solution)/shard_map/pallas_call | solution.py:464
  94.4 0.6 copy.8

commit v6 on v5

--- a/solution.py
+++ b/solution.py
@@ -62,10 +62,7 @@
         )
     ]
     b_in[0].start()
-    for copy in small_in:
-        copy.start()
-    b_in[1].start()
-    b_in[2].start()
+    small_in[0].start()
 
     barrier = pltpu.get_barrier_semaphore()
 
@@ -86,7 +83,7 @@
             target[lam0 + l] = source_rows[pl.ds(l, rows, stride=stride), :].astype(BF16)
             return carry
 
-        lax.fori_loop(0, tile, body, 0, unroll=8)
+        lax.fori_loop(0, tile, body, 0, unroll=16)
 
     def widen_b(j):
         flag = tm_ref[0, j].astype(F32)
@@ -97,10 +94,12 @@
             )
             return carry
 
-        lax.fori_loop(0, rows, body, 0)
+        lax.fori_loop(0, rows, body, 0, unroll=2)
 
     small_in[0].wait()
     b_in[0].wait()
+    for copy in small_in[1:] + b_in[1:]:
+        copy.start()
     widen_b(0)
     regroup(wide, tile, bt, 0)
 

time: 95.4 us -> 95.5 us (level)
  no operation moved by 1% of the time
where the time goes in v6:
time: 95.5 us; the launch traced here: 95 us
  Pallas kernels  94.4 us (99%)
    pallas_call x1, Pallas kernels, per_device(): pl.pallas_call(functools.partial(kernel, n_ao, n_ri, n_x, n_z, tile, rows...  94.4 us

profile of v6, /device:TPU:1, one launch (start us, length us, event | category | flops | bytes accessed | tf_op | source)
XLA Modules:
  0.0 95.0 jit_solution(8390767202340579669)
XLA Ops:
  0.0 94.4 %shard_map.64 = f32[16,256]{1,0:T(8,128)S(1)} custom-call(bf16[16,384,128]{2,1,0:T(8,128)(2,1)} %b_hbm.1, bf16[128,640]{1,0:T(8,128)(2,1)} %occ_hbm.1, bf16[128,384]{1,0:T(8,128)(2,1)} %virt_hbm.1, s32[1,3]{1,0:T(1,128)} %tm_hbm.1, s32[1,5]{1,0:T(1,128)} %om_hbm.1, s32[1,3]{1,0:T(1,128)} %vm_hbm.1), custom_call_target="tpu_custom_call" | custom-call | tf_op jit(solution)/shard_map/pallas_call | solution.py:463
  94.4 0.6 copy.8

commit v7 on v6

--- a/solution.py
+++ b/solution.py
@@ -61,8 +61,16 @@
             ((tm_hbm, tm_ref), (om_hbm, om_ref), (vm_hbm, vm_ref), (occ_hbm, occ_ref), (virt_hbm, virt_ref))
         )
     ]
-    b_in[0].start()
+    half_tile = tile // 2
+    b_first = [
+        pltpu.make_async_copy(
+            b_hbm.at[:, pl.ds(h * half_tile, half_tile), :], b_ref.at[:, pl.ds(h * half_tile, half_tile), :], sem
+        )
+        for h, sem in ((0, in_sem.at[0]), (1, in_sem.at[8]))
+    ]
     small_in[0].start()
+    for copy in b_first:
+        copy.start()
 
     barrier = pltpu.get_barrier_semaphore()
 
@@ -78,30 +86,32 @@
     for where in [right, left, z_peer(1), z_peer(n_z - 1)] + [x_peer(d) for d in x_beside]:
         greet({"ao": where})
 
-    def regroup(source_rows, stride, target, lam0):
+    def regroup(source_rows, stride, target, lam0, first=0, count=tile):
         def body(l, carry):
             target[lam0 + l] = source_rows[pl.ds(l, rows, stride=stride), :].astype(BF16)
             return carry
 
-        lax.fori_loop(0, tile, body, 0, unroll=16)
-
-    def widen_b(j):
+        lax.fori_loop(first, first + count, body, 0, unroll=16)
+
+    def widen_b(j, first=0, count=tile):
         flag = tm_ref[0, j].astype(F32)
 
         def body(p, carry):
-            wide[pl.ds(pl.multiple_of(p * tile, tile), tile), :] = (
-                b_ref[p, pl.ds(j * tile, tile), :].astype(F32) * flag
+            wide[pl.ds(pl.multiple_of(p * tile + first, count), count), :] = (
+                b_ref[p, pl.ds(j * tile + first, count), :].astype(F32) * flag
             )
             return carry
 
         lax.fori_loop(0, rows, body, 0, unroll=2)
 
     small_in[0].wait()
-    b_in[0].wait()
-    for copy in small_in[1:] + b_in[1:]:
-        copy.start()
-    widen_b(0)
-    regroup(wide, tile, bt, 0)
+    for h in range(2):
+        b_first[h].wait()
+        if h == 1:
+            for copy in small_in[1:] + b_in[1:]:
+                copy.start()
+        widen_b(0, h * half_tile, half_tile)
+        regroup(wide, tile, bt, 0, h * half_tile, half_tile)
 
     pl.semaphore_wait(barrier, 5 + 4 + len(x_beside))
 
@@ -490,7 +500,7 @@
                 pltpu.VMEM((n_ri // 2, rows, size), BF16),
                 pltpu.VMEM((n_x, rows, size), F32),
                 pltpu.VMEM((n_z, rows, size), BF16),
-                dma((8,)),
+                dma((9,)),
                 pltpu.SemaphoreType.REGULAR((3,)),
                 pltpu.SemaphoreType.REGULAR((2,)),
                 pltpu.SemaphoreType.REGULAR((3,)),

time: 95.5 us -> 95.5 us (level)
  no operation moved by 1% of the time
where the time goes in v7:
time: 95.5 us; the launch traced here: 95.1 us
  Pallas kernels  94.4 us (99%)
    pallas_call x1, Pallas kernels, per_device(): pl.pallas_call(functools.partial(kernel, n_ao, n_ri, n_x, n_z, tile, rows...  94.4 us

profile of v7, /device:TPU:1, one launch (start us, length us, event | category | flops | bytes accessed | tf_op | source)
XLA Modules:
  0.0 95.1 jit_solution(11228909770863999542)
XLA Ops:
  0.0 94.4 %shard_map.64 = f32[16,256]{1,0:T(8,128)S(1)} custom-call(bf16[16,384,128]{2,1,0:T(8,128)(2,1)} %b_hbm.1, bf16[128,640]{1,0:T(8,128)(2,1)} %occ_hbm.1, bf16[128,384]{1,0:T(8,128)(2,1)} %virt_hbm.1, s32[1,3]{1,0:T(1,128)} %tm_hbm.1, s32[1,5]{1,0:T(1,128)} %om_hbm.1, s32[1,3]{1,0:T(1,128)} %vm_hbm.1), custom_call_target="tpu_custom_call" | custom-call | tf_op jit(solution)/shard_map/pallas_call | solution.py:473
  94.4 0.6 copy.8
